TPU v7x, 32 devices: a whole 2x2x4 slice. The times are simulated.
32 devices in a mesh: groups: 2 (over y), gy: 4 (over z), gz: 4 (over x, core).
Axes of the slice: x: 2, y: 2, z: 4, core: 2. Of those that a mesh axis runs over, the one named last changes fastest.
Arguments:
- indirect: float32 [4, 512, 32, 512], P('groups', 'gy', 'gz'), parts along dimension 0, may hold values from -6 to 6
- past_indirect: float32 [8, 2, 512, 32, 512], P('groups', None, 'gy', 'gz'), parts along dimension 0, may hold values from -6 to 6
- past_residual: float32 [8, 2, 512, 32, 512], P('groups', None, 'gy', 'gz'), parts along dimension 0, may hold values from -40 to 40
- atom_table: float32 [10, 4, 4, 128], P('groups', 'gy', 'gz'), parts along dimension 0, may hold values from -4 to 512, as said below
- atom_counts: int32 [8, 4], P(('groups', 'gy'), 'gz'), parts along dimension 0, may hold values from 1 to 128, as said below
- chi_amps: float32 [3, 4], replicated, may hold values from -3 to 3
- chi_widths: float32 [4], replicated, may hold values from 0.5 to 4
Outputs:
- new_indirect: float32 [4, 512, 32, 512], P('groups', 'gy', 'gz'), parts along dimension 0
- residual: float32 [4, 512, 32, 512], P('groups', 'gy', 'gz'), parts along dimension 0
There are 2 independent parts, one for each index of `groups`. A program takes and returns all parts, laid end to end along the dimension named above; an argument that names none is the same for every part. Nothing has to cross between parts.
Inputs may be any that keep to these rules, and one draw needn't show every extreme that they name: `atom_counts`: some pencil has exactly 128 live rows in every draw. `atom_table`: each row of pencil (p, q) has its y position in [p * 128, (p + 1) * 128) and its z position in [q * 8, (q + 1) * 8); x positions lie in [0, 512).
All inputs are finite; a program needn't handle non-finite values.
Results may differ from a plain program's by a relative error of at most 0.0003.
Values sent between devices are 32-bit elements; how exact they have to be, the bound alone decides.
A program may use at most 192 MiB of HBM per device.

v0:
```python
import math
import jax
import jax.numpy as jnp
from jax import lax
from jax.sharding import PartitionSpec as P

SIGX = 8
PRECISE = lax.Precision.HIGHEST
MIX_STEP = 0.3
BOND_OH = 1.9
BOND_HH = 3.1


def with_halo(cells, sides, width):
    for axis, dim in sides:
        count = lax.axis_size(axis)
        head = lax.slice_in_dim(cells, 0, width, axis=dim)
        tail = lax.slice_in_dim(cells, cells.shape[dim] - width, cells.shape[dim], axis=dim)
        cells = jnp.concatenate(
            [
                lax.ppermute(tail, axis, [(i, (i + 1) % count) for i in range(count)]),
                cells,
                lax.ppermute(head, axis, [((i + 1) % count, i) for i in range(count)]),
            ],
            axis=dim,
        )
    return cells


def hartley(length):
    position = lax.iota(jnp.int32, length)
    product = position[:, None] * position[None, :] % length
    angle = product.astype(jnp.float32) * (2.0 * math.pi / length)
    return (jnp.cos(angle) + jnp.sin(angle)) / math.sqrt(length)


def wave_squared(position, length):
    folded = jnp.where(2 * position > length, position - length, position)
    scaled = folded.astype(jnp.float32) * (2.0 * math.pi / length)
    return scaled * scaled


def response(wave_square, chi_amps, chi_widths):
    wavenumber = jnp.sqrt(wave_square)
    summed = [jnp.zeros_like(wave_square) for channel in range(3)]
    for which_term in range(chi_widths.shape[0]):
        gaussian_term = jnp.exp(-wave_square * (chi_widths[which_term] * chi_widths[which_term]))
        summed = [
            summed[channel] + chi_amps[channel, which_term] * gaussian_term for channel in range(3)
        ]
    oxygen = 1.0 + summed[0]
    mixed_site = 2.0 * jnp.sinc(wavenumber * (BOND_OH / math.pi)) + summed[1]
    hydrogen = 2.0 + 2.0 * jnp.sinc(wavenumber * (BOND_HH / math.pi)) + summed[2]
    return (oxygen, mixed_site, hydrogen)


def couple(spectrum, wave_square, chi_amps, chi_widths):
    oxygen, mixed_site, hydrogen = response(wave_square, chi_amps, chi_widths)
    return jnp.stack(
        [
            oxygen * spectrum[0] + mixed_site * spectrum[1],
            mixed_site * spectrum[0] + hydrogen * spectrum[1],
        ]
    )


def gaussian(offset, length, spread):
    offset = offset - length * jnp.floor(offset / length + 0.5)
    return jnp.exp(-0.5 * offset * offset / (spread * spread))


def pencil_field(
    atom_rows, pencil_y, pencil_z, cells_y, cells_z, total_x, total_y, total_z, spread_x
):
    cell_y = (pencil_y * cells_y + lax.iota(jnp.int32, cells_y)).astype(jnp.float32)
    cell_z = (pencil_z * cells_z + lax.iota(jnp.int32, cells_z)).astype(jnp.float32)
    cell_x = lax.iota(jnp.int32, total_x).astype(jnp.float32)
    along_y = gaussian(cell_y[:, None] - atom_rows[1][None, :], total_y, 0.5 * cells_y)
    along_z = gaussian(cell_z[:, None] - atom_rows[2][None, :], total_z, 0.5 * cells_z)
    along_x = gaussian(cell_x[:, None] - atom_rows[0][None, :], total_x, spread_x)
    left = atom_rows[3:5][:, None, None, :] * along_y[None, :, None, :] * along_z[None, None, :, :]
    left = left.reshape(2, cells_y * cells_z, atom_rows.shape[1])
    return jnp.einsum("sra,xa->srx", left, along_x, precision=PRECISE)


def body(indirect, past_indirect, past_residual, atom_table, atom_counts, chi_amps, chi_widths):
    cells_y = indirect.shape[1]
    cells_z = indirect.shape[2]
    cells_x = indirect.shape[3]
    parts_y = lax.axis_size("gy")
    parts_z = lax.axis_size("gz")
    total_y = cells_y * parts_y
    total_z = cells_z * parts_z
    row_count = atom_table.shape[3]
    present = (lax.iota(jnp.int32, row_count) < atom_counts[0, 0]).astype(jnp.float32)
    bucket = jnp.concatenate([atom_table[0:3], atom_table[3:5] * present], 0)
    nearby = with_halo(bucket, (("gy", 1), ("gz", 2)), 1)
    nearby = nearby.reshape(5, 9 * row_count)
    potential_field = pencil_field(
        nearby,
        lax.axis_index("gy"),
        lax.axis_index("gz"),
        cells_y,
        cells_z,
        cells_x,
        total_y,
        total_z,
        float(SIGX),
    )
    potential_field = potential_field.reshape(2, cells_y, cells_z, cells_x)
    argument = indirect - potential_field
    closed = jnp.where(argument > 0, argument, jnp.expm1(jnp.minimum(argument, 0.0)))
    direct = closed - indirect
    table_x = hartley(cells_x)
    table_y = hartley(total_y)
    table_z = hartley(total_z)
    blocks = parts_y * parts_z
    width_x = cells_x // blocks
    grid_y = table_y.reshape(parts_y, cells_y, total_y)
    grid_z = table_z.reshape(parts_z, cells_z, total_z)
    outgoing = jnp.einsum(
        "scdx,xqk->sqkdc", direct, table_x.reshape(cells_x, blocks, width_x), precision=PRECISE
    )
    outgoing = outgoing.reshape(2, blocks, 1, width_x * cells_z * cells_y)
    received = lax.all_to_all(outgoing, ("gy", "gz"), split_axis=1, concat_axis=2, tiled=True)
    count = received.shape[0]
    pieces = received.reshape(count, parts_y, parts_z, width_x, cells_z, cells_y)
    partial_value = jnp.einsum("sabxdc,acy->sbxdy", pieces, grid_y, precision=PRECISE)
    section_two = jnp.einsum("sbxdy,bdz->sxzy", partial_value, grid_z, precision=PRECISE)
    wave_x = wave_squared(
        lax.axis_index(("gy", "gz")) * width_x + lax.iota(jnp.int32, width_x), cells_x
    )
    wave_square = (
        wave_x[:, None, None]
        + wave_squared(lax.iota(jnp.int32, total_z), total_z)[None, :, None]
        + wave_squared(lax.iota(jnp.int32, total_y), total_y)[None, None, :]
    )
    coupled = couple(section_two, wave_square, chi_amps, chi_widths)
    partial_value = jnp.einsum("sxzy,bdz->sxbdy", coupled, grid_z, precision=PRECISE)
    returning = jnp.einsum("sxbdy,acy->sabxdc", partial_value, grid_y, precision=PRECISE)
    returning = returning.reshape(2, blocks, 1, width_x * cells_z * cells_y)
    table_back = table_x.reshape(blocks, width_x, cells_x)
    received = lax.all_to_all(returning, ("gy", "gz"), split_axis=1, concat_axis=2, tiled=True)
    count = received.shape[0]
    pieces = received.reshape(count, blocks, width_x, cells_z, cells_y)
    summed_field = jnp.einsum("sqxdc,qxk->scdk", pieces, table_back, precision=PRECISE)
    residual = summed_field - direct - indirect
    stacked = jnp.concatenate([residual[None], past_residual], 0)
    gram_matrix = jnp.einsum("isyzx,jsyzx->ij", stacked, stacked, precision=PRECISE)
    gram_matrix = lax.psum(gram_matrix, ("gy", "gz"))
    factor = jnp.linalg.cholesky(gram_matrix)
    weights = jax.scipy.linalg.cho_solve(
        (factor, True), jnp.ones((gram_matrix.shape[0],), jnp.float32)
    )
    mixing = weights / jnp.sum(weights)
    earlier = jnp.einsum(
        "i,isyzx->syzx", mixing[1:], past_indirect + MIX_STEP * past_residual, precision=PRECISE
    )
    new_indirect = mixing[0] * (indirect + MIX_STEP * residual) + earlier
    return (new_indirect, residual)


def solution(mesh):
    return jax.shard_map(
        body,
        mesh=mesh,
        in_specs=(
            P("groups", "gy", "gz", None),
            P("groups", None, "gy", "gz", None),
            P("groups", None, "gy", "gz", None),
            P("groups", "gy", "gz", None),
            P(("groups", "gy"), "gz"),
            P(),
            P(),
        ),
        out_specs=(P("groups", "gy", "gz", None), P("groups", "gy", "gz", None)),
        check_vma=False,
    )
```

profile of v0, /device:TPU:0, one launch (start us, length us, event | category | flops | bytes accessed | tf_op | source)
XLA Modules:
  0.0 549.4 jit_solution(14519221556603764568)
XLA Ops:
  1.3 0.7 slice.114
  2.0 0.7 slice_multiply_fusion
  2.7 3.1 collective-permute-start
  5.7 2.1 collective-permute-start.1
  7.8 1.5 collective-permute-done
  9.4 1.7 collective-permute-start.3
  11.2 1.3 collective-permute-done.2
  12.6 0.3 fusion.195
  12.9 0.1 broadcast_multiply_fusion
  13.0 0.1 fusion.224
  13.1 18.8 %fusion.6 = f32[2,128,8,512]{3,1,2,0:T(8,128)S(1)} fusion(f32[8,1152]{1,0:T(8,128)S(1)} %fusion.224, f32[2,128,1152]{2,1,0:T(8,128)S(1)} %broadcast_multiply_fusion, f32[1152]{0:T(1024)S(1)} %sub.111, f32[512]{0:T(512)S(1)} %iota_convert_fusion), kind=kOutput, calls=%fused_computation.8 | convolution fusion | flops 14503182336 | bytes 5417472 | tf_op jit(solution)/shard_map/sra,xa->srx/dot_general | solution.py:83
  31.9 14.1 %fusion.56 = f32[2,16,32,8,128]{4,2,3,0,1:T(8,128)S(1)} fusion(f32[2,128,8,512]{3,1,2,0:T(8,128)S(1)} %fusion.6, f32[2,128,8,512]{3,2,1,0:T(8,128)S(1)} %copy-done.2, s32[16,32]{1,0:T(8,128)S(1)} %multiply_add_fusion.3), kind=kOutput, calls=%fused_computation.68 | convolution fusion | flops 6451888128 | bytes 12584960 | tf_op jit(solution)/shard_map/scdx,xqk->sqkdc/dot_general | solution.py:121
  46.0 5.8 %copy.90 = f32[2,16,32,8,128]{4,3,2,0,1:T(8,128)} copy(f32[2,16,32,8,128]{4,2,3,0,1:T(8,128)S(1)} %fusion.56) | data formatting | bytes 8388608 | tf_op jit(solution)/shard_map/reshape | solution.py:124
  51.8 5.9 %reshape.439 = f32[2,16,1,32768]{3,0,2,1:T(2,128)} reshape(f32[2,16,32,8,128]{4,3,2,0,1:T(8,128)} %copy.90) | data formatting | bytes 8388608 | tf_op jit(solution)/shard_map/reshape | solution.py:124
  57.8 6.7 %all-to-all-start = ((f32[2,16,1,32768]{3,0,2,1:T(2,128)}), f32[2,16,1,32768]{3,0,2,1:T(2,128)}, u32[]{:S(2)}, u32[]{:S(2)}) async-start(f32[2,16,1,32768]{3,0,2,1:T(2,128)} %reshape.439), calls=%async_computation | async-start | bytes 8388608 | tf_op jit(solution)/shard_map/all_to_all | solution.py:125
  64.5 0.7 fusion.287
  70.3 0.7 fusion.286
  71.0 71.0 %all-to-all-done = f32[2,16,1,32768]{3,0,2,1:T(2,128)} async-done(((f32[2,16,1,32768]{3,0,2,1:T(2,128)}), f32[2,16,1,32768]{3,0,2,1:T(2,128)}, u32[]{:S(2)}, u32[]{:S(2)}) %all-to-all-start) | async-done | bytes 4194336 | tf_op jit(solution)/shard_map/all_to_all | solution.py:125
  142.1 7.0 %reshape.440 = f32[2,4,4,32,8,128]{5,4,3,0,2,1:T(8,128)} reshape(f32[2,16,1,32768]{3,0,2,1:T(2,128)} %all-to-all-done) | data formatting | bytes 8388608 | tf_op jit(solution)/shard_map/reshape | solution.py:127
  149.1 13.7 %fusion.21 = f32[2,4,32,8,512,1]{4,3,5,1,2,0:T(8,128)S(1)} fusion(f32[2,4,4,32,8,128]{5,4,3,0,2,1:T(8,128)} %reshape.440, s32[4,128]{1,0:T(4,128)S(1)} %multiply_add_fusion.5), kind=kOutput, calls=%fused_computation.26 | convolution fusion | flops 6446645248 | bytes 8390656 | tf_op jit(solution)/shard_map/sabxdc,acy->sbxdy/dot_general | solution.py:128
  162.8 4.3 fusion.59
  167.2 12.9 %fusion.101 = f32[1,32,32,512]{3,2,1,0:T(8,128)S(1)} fusion(f32[2,32,32,512]{3,2,1,0:T(8,128)S(1)} %fusion.59, f32[]{:T(128)} %bitcast.42, f32[]{:T(128)} %bitcast.41, f32[]{:T(128)} %bitcast.40, f32[]{:T(128)} %bitcast.39, f32[]{:T(128)} %bitcast.14, f32[]{:T(128)} %bitcast.12, f32[]{:T(128)} %bitcast.10, f32[]{:T(128)} %bitcast.8, f32[512]{0:T(512)S(1)} %fusion.240, ...), kind=kLoop, calls=%fused_computation.107 | loop fusion | flops 50331648 | bytes 6297648 | tf_op jit(solution)/shard_map/stack | solution.py:59
  180.0 10.3 %fusion.90 = f32[1,32,32,512]{3,2,1,0:T(8,128)S(1)} fusion(f32[2,32,32,512]{3,2,1,0:T(8,128)S(1)} %fusion.59, f32[]{:T(128)} %bitcast.14, f32[]{:T(128)} %bitcast.13, f32[]{:T(128)} %bitcast.12, f32[]{:T(128)} %bitcast.11, f32[]{:T(128)} %bitcast.10, f32[]{:T(128)} %bitcast.9, f32[]{:T(128)} %bitcast.8, f32[512]{0:T(512)S(1)} %fusion.240, ...), kind=kLoop, calls=%fused_computation.96 | loop fusion | flops 31457280 | bytes 6297648 | tf_op jit(solution)/shard_map/stack | solution.py:59
  190.4 4.1 fusion.62
  194.5 13.6 %fusion.63 = f32[2,4,4,32,8,128]{5,3,4,2,0,1:T(8,128)S(1)} fusion(f32[2,32,4,8,512]{4,3,1,0,2:T(8,128)S(1)} %fusion.62, s32[4,128]{1,0:T(4,128)S(1)} %multiply_add_fusion.5), kind=kOutput, calls=%fused_computation.71 | convolution fusion | flops 6446645248 | bytes 8390656 | tf_op jit(solution)/shard_map/sxbdy,acy->sabxdc/dot_general | solution.py:140
  208.0 5.8 %copy.93 = f32[2,4,4,32,8,128]{5,4,3,0,2,1:T(8,128)} copy(f32[2,4,4,32,8,128]{5,3,4,2,0,1:T(8,128)S(1)} %fusion.63) | data formatting | bytes 8388608 | tf_op jit(solution)/shard_map/reshape | solution.py:141
  213.8 5.9 %reshape.441 = f32[2,16,1,32768]{3,0,2,1:T(2,128)} reshape(f32[2,4,4,32,8,128]{5,4,3,0,2,1:T(8,128)} %copy.93) | data formatting | bytes 8388608 | tf_op jit(solution)/shard_map/reshape | solution.py:141
  219.7 19.7 %all-to-all-start.1 = ((f32[2,16,1,32768]{3,0,2,1:T(2,128)}), f32[2,16,1,32768]{3,0,2,1:T(2,128)}, u32[]{:S(2)}, u32[]{:S(2)}) async-start(f32[2,16,1,32768]{3,0,2,1:T(2,128)} %reshape.441), calls=%async_computation.1 | async-start | bytes 8388608 | tf_op jit(solution)/shard_map/all_to_all | solution.py:143
  239.4 18.3 %copy.69 = f32[4,2,128,8,512]{2,0,3,4,1:T(4,128)} copy(f32[4,2,128,8,512]{4,3,2,1,0:T(8,128)} %param.10) | data formatting | bytes 33554432 | tf_op args[2]
  257.7 17.5 %multiply_add_fusion = f32[4,2,128,8,512]{4,3,2,1,0:T(8,128)} fusion(f32[4,2,128,8,512]{4,3,2,1,0:T(8,128)} %param.9, f32[4,2,128,8,512]{4,3,2,1,0:T(8,128)} %param.10), kind=kLoop, calls=%fused_computation.6 | loop fusion | flops 8388608 | bytes 50331648 | tf_op jit(solution)/shard_map/add | solution.py:157
  275.2 41.7 %all-to-all-done.1 = f32[2,16,1,32768]{3,0,2,1:T(2,128)} async-done(((f32[2,16,1,32768]{3,0,2,1:T(2,128)}), f32[2,16,1,32768]{3,0,2,1:T(2,128)}, u32[]{:S(2)}, u32[]{:S(2)}) %all-to-all-start.1) | async-done | bytes 4194336 | tf_op jit(solution)/shard_map/all_to_all | solution.py:143
  317.0 6.6 %reshape.442 = f32[2,16,32,8,128]{4,3,2,0,1:T(8,128)} reshape(f32[2,16,1,32768]{3,0,2,1:T(2,128)} %all-to-all-done.1) | data formatting | bytes 8388608 | tf_op jit(solution)/shard_map/reshape | solution.py:145
  323.6 26.4 %fusion.14 = f32[2,128,8,512]{3,1,2,0:T(8,128)S(1)} fusion(f32[2,128,8,512]{3,2,1,0:T(8,128)} %param.8, f32[2,128,8,512]{3,1,2,0:T(8,128)} %copy-done.6, f32[2,16,32,8,128]{4,3,2,0,1:T(8,128)} %reshape.442, s32[16,32]{1,0:T(8,128)S(1)} %multiply_add_fusion.3), kind=kOutput, calls=%fused_computation.18 | convolution fusion | flops 6453985280 | bytes 16779264 | tf_op jit(solution)/shard_map/sqxdc,qxk->scdk/dot_general | solution.py:146
  350.0 4.4 copy.75
  354.4 11.0 %copy.68 = f32[1,2,128,8,512]{2,0,3,4,1:T(1,128)} copy(f32[1,2,128,8,512]{4,2,3,1,0:T(8,128)} %bitcast.155) | data formatting | bytes 8388608 | tf_op jit(solution)/shard_map/broadcast_in_dim | solution.py:148
  365.4 76.1 %fusion.132 = f32[5,5]{0,1:T(8,128)S(1)} fusion(f32[4,2,128,8,512]{2,0,3,4,1:T(4,128)} %copy.69, f32[1,2,128,8,512]{2,0,3,4,1:T(1,128)} %copy.68), kind=kOutput, calls=%fused_computation.158 | convolution fusion | flops 319815680 | bytes 20971620 | tf_op jit(solution)/shard_map/isyzx,jsyzx->ij/dot_general | solution.py:149
  441.5 47.8 %psum.7 = f32[5,5]{0,1:T(8,128)S(1)} all-reduce(f32[5,5]{0,1:T(8,128)S(1)} %fusion.132), channel_id=1, replica_groups=mesh['groups'=2,'gy'=4,'gz'=4] {'gy','gz'}, use_global_device_ids=true, to_apply=%region_0.2 | all-reduce | flops 25 | bytes 200 | tf_op jit(solution)/shard_map/psum | solution.py:150
  489.2 0.1 copy.71
  489.3 0.4 cholesky.16
  489.8 0.6 compare_reduce_fusion
  490.4 0.5 fusion.233
  491.0 0.4 custom-call.10
  491.4 0.1 convolution_bitcast_fusion.1
  491.5 0.7 fusion.288
  492.2 0.5 broadcast_divide_fusion
  492.8 46.8 %fusion.4 = f32[1,2,128,8,512]{4,0,3,2,1:T(1,128)S(1)} fusion(f32[4,2,128,8,512]{4,3,2,1,0:T(8,128)} %multiply_add_fusion, f32[5]{0:T(128)S(1)} %broadcast_divide_fusion), kind=kOutput, calls=%fused_computation.4 | convolution fusion | flops 50331648 | bytes 20971540 | tf_op jit(solution)/shard_map/i,isyzx->syzx/dot_general | solution.py:156
  539.6 5.1 bitcast_add_fusion
  544.8 4.4 copy.74
  (38 shorter events, 0.4 us)
Async XLA Ops:
  2.7 6.7 %collective-permute-start = (f32[5,1,1,128]{3,2,1,0:T(1,128)S(1)}, f32[5,1,1,128]{3,2,1,0:T(1,128)S(1)}, u32[]{:S(2)}, u32[]{:S(2)}) collective-permute-start(f32[5,1,1,128]{3,2,1,0:T(1,128)S(1)} %pad_maximum_fusion.5), channel_id=1, source_target_pairs={{0,4},{4,8},{8,12},{12,0},{1,5},{5,9},{9,13},{13,1},{2,6},{6,10},{... | collective-permute-start | bytes 7688 | tf_op jit(solution)/shard_map/ppermute | solution.py:21
  5.7 3.6 collective-permute-start.1
  9.3 3.1 collective-permute-start.2
  9.4 3.1 collective-permute-start.3
  13.1 18.8 %copy-start.2 = (f32[2,128,8,512]{3,2,1,0:T(8,128)S(1)}, f32[2,128,8,512]{3,2,1,0:T(8,128)}, u32[]{:S(2)}) copy-start(f32[2,128,8,512]{3,2,1,0:T(8,128)} %param.8) | copy-start | bytes 12582916
  31.9 14.1 %copy-start.6 = (f32[2,128,8,512]{3,1,2,0:T(8,128)}, f32[2,128,8,512]{3,1,2,0:T(8,128)S(1)}, u32[]{:S(2)}) copy-start(f32[2,128,8,512]{3,1,2,0:T(8,128)S(1)} %fusion.6) | copy-start | bytes 12582916
  57.7 6.8 %copy-start.5 = (f32[4]{0:T(128)S(1)}, f32[4]{0:T(128)}, u32[]{:S(2)}) copy-start(f32[4]{0:T(128)} %param.14) | copy-start | bytes 52
  57.8 12.5 %copy-start.4 = (f32[3,4]{1,0:T(4,128)S(1)}, f32[3,4]{1,0:T(4,128)}, u32[]{:S(2)}) copy-start(f32[3,4]{1,0:T(4,128)} %param.13) | copy-start | bytes 148
  57.8 84.3 %all-to-all-start = ((f32[2,16,1,32768]{3,0,2,1:T(2,128)}), f32[2,16,1,32768]{3,0,2,1:T(2,128)}, u32[]{:S(2)}, u32[]{:S(2)}) async-start(f32[2,16,1,32768]{3,0,2,1:T(2,128)} %reshape.439), calls=%async_computation | async-start | bytes 8388608 | tf_op jit(solution)/shard_map/all_to_all | solution.py:125
  219.7 97.2 %all-to-all-start.1 = ((f32[2,16,1,32768]{3,0,2,1:T(2,128)}), f32[2,16,1,32768]{3,0,2,1:T(2,128)}, u32[]{:S(2)}, u32[]{:S(2)}) async-start(f32[2,16,1,32768]{3,0,2,1:T(2,128)} %reshape.441), calls=%async_computation.1 | async-start | bytes 8388608 | tf_op jit(solution)/shard_map/all_to_all | solution.py:143
  350.0 4.5 copy-start
  492.8 46.8 %copy-start.1 = (f32[2,128,8,512]{3,1,2,0:T(8,128)S(1)}, f32[2,128,8,512]{3,1,2,0:T(8,128)}, u32[]{:S(2)}) copy-start(f32[2,128,8,512]{3,1,2,0:T(8,128)} %copy-done) | copy-start | bytes 12582916
  492.8 46.8 %copy-start.3 = (f32[2,128,8,512]{3,2,1,0:T(8,128)S(1)}, f32[2,128,8,512]{3,2,1,0:T(8,128)}, u32[]{:S(2)}) copy-start(f32[2,128,8,512]{3,2,1,0:T(8,128)} %param.8) | copy-start | bytes 12582916
where the time goes:
time: 558 us; the launch traced here: 549 us
  matrix products  219 us (39%)
  waiting for transfers between devices  116 us (21%)
  local copies, waits for them, and re-layouts  77.4 us (14%)
  other arithmetic  49.8 us (9%)
  blocking collectives  47.8 us (9%)
  starting transfers between devices  33.4 us (6%)
  between operations  6.84 us (1%)
    dot_general x1, matrix products, body(): jnp.einsum('isyzx,jsyzx->ij', stacked, stacked, precision=PRECISE)  76.1 us
    all_to_all x1, waiting for transfers between devices, body(): lax.all_to_all(outgoing, ('gy', 'gz'), split_axis=1, concat_axis=2, tiled...  71 us
    psum x1, blocking collectives, body(): gram_matrix = lax.psum(gram_matrix, ('gy', 'gz'))  47.8 us
    dot_general x1, matrix products, body(): jnp.einsum('i,isyzx->syzx', mixing[1:], past_indirect + MIX_STEP * past_r...  46.8 us
    all_to_all x1, waiting for transfers between devices, body(): lax.all_to_all(returning, ('gy', 'gz'), split_axis=1, concat_axis=2, tile...  41.7 us
    unnamed x17, local copies, waits for them, and re-layouts  27.2 us
    dot_general x1, matrix products, body(): jnp.einsum('sqxdc,qxk->scdk', pieces, table_back, precision=PRECISE)  26.4 us
    another operation x2, other arithmetic, couple(): jnp.stack([oxygen * spectrum[0] + mixed_site * spectrum[1], mixed_site *...  23.2 us
  transfers between devices with their start and end apart: 6, of which 4 were waited for; matrix products, arithmetic and copies ran while one was open for 7% of the time, Pallas kernels for 0%

commit v1 on v0

--- a/solution.py
+++ b/solution.py
@@ -122,7 +122,9 @@
         "scdx,xqk->sqkdc", direct, table_x.reshape(cells_x, blocks, width_x), precision=PRECISE
     )
     outgoing = outgoing.reshape(2, blocks, 1, width_x * cells_z * cells_y)
-    received = lax.all_to_all(outgoing, ("gy", "gz"), split_axis=1, concat_axis=2, tiled=True)
+    parts = jnp.split(outgoing, lax.axis_size(("gy", "gz")), axis=1)
+    got = lax.all_to_all(jnp.stack(parts), ("gy", "gz"), 0, 0)
+    received = jnp.concatenate(got, axis=2)
     count = received.shape[0]
     pieces = received.reshape(count, parts_y, parts_z, width_x, cells_z, cells_y)
     partial_value = jnp.einsum("sabxdc,acy->sbxdy", pieces, grid_y, precision=PRECISE)

time: 558 us -> 578 us (1.036)
  local copies, waits for them, and re-layouts: 77.4 us -> 97 us
    unnamed x17 -> x34, local copies, waits for them, and re-layouts: 27.2 us -> 53.8 us
    reshape x1 -> x0, local copies, waits for them, and re-layouts: 7.04 us -> none  [body(): received.reshape(count, parts_y, parts_z, width_x, cells_z, cells_y)]
    reshape x2 -> x1, local copies, waits for them, and re-layouts: 11.7 us -> 4.94 us  [body(): outgoing = outgoing.reshape(2, blocks, 1, width_x * cells_z * cells_y)]
    transpose x0 -> x1, local copies, waits for them, and re-layouts: none -> 5.81 us  [body(): jnp.einsum('scdx,xqk->sqkdc', direct, table_x.reshape(cells_x, blocks, wi...]
where the time goes in v1:
time: 578 us; the launch traced here: 570 us
  matrix products  219 us (38%)
  waiting for transfers between devices  115 us (20%)
  local copies, waits for them, and re-layouts  97 us (17%)
  other arithmetic  50.4 us (9%)
  blocking collectives  47.7 us (8%)
  starting transfers between devices  33.8 us (6%)
  between operations  7.04 us (1%)
    dot_general x1, matrix products, body(): jnp.einsum('isyzx,jsyzx->ij', stacked, stacked, precision=PRECISE)  76.1 us
    all_to_all x1, waiting for transfers between devices, body(): got = lax.all_to_all(jnp.stack(parts), ('gy', 'gz'), 0, 0)  70.3 us
    unnamed x34, local copies, waits for them, and re-layouts  53.8 us
    psum x1, blocking collectives, body(): gram_matrix = lax.psum(gram_matrix, ('gy', 'gz'))  47.7 us
    dot_general x1, matrix products, body(): jnp.einsum('i,isyzx->syzx', mixing[1:], past_indirect + MIX_STEP * past_r...  46.8 us
    all_to_all x1, waiting for transfers between devices, body(): lax.all_to_all(returning, ('gy', 'gz'), split_axis=1, concat_axis=2, tile...  41.7 us
    dot_general x1, matrix products, body(): jnp.einsum('sqxdc,qxk->scdk', pieces, table_back, precision=PRECISE)  26.4 us
    another operation x2, other arithmetic, couple(): jnp.stack([oxygen * spectrum[0] + mixed_site * spectrum[1], mixed_site *...  23.6 us
  transfers between devices with their start and end apart: 6, of which 4 were waited for; matrix products, arithmetic and copies ran while one was open for 7% of the time, Pallas kernels for 0%

profile of v1, /device:TPU:0, one launch (start us, length us, event | category | flops | bytes accessed | tf_op | source)
XLA Modules:
  0.0 569.6 jit_solution(10481851244231089377)
XLA Ops:
  2.7 3.1 collective-permute-start
  5.7 2.1 collective-permute-start.1
  7.8 1.5 collective-permute-done
  9.4 1.7 collective-permute-start.3
  11.2 1.3 collective-permute-done.2
  13.1 18.8 %fusion.6 = f32[2,128,8,512]{3,1,2,0:T(8,128)S(1)} fusion(f32[8,1152]{1,0:T(8,128)S(1)} %fusion.240, f32[2,128,1152]{2,1,0:T(8,128)S(1)} %broadcast_multiply_fusion, f32[1152]{0:T(1024)S(1)} %sub.111, f32[512]{0:T(512)S(1)} %iota_convert_fusion), kind=kOutput, calls=%fused_computation.8 | convolution fusion | flops 14503182336 | bytes 5417472 | tf_op jit(solution)/shard_map/sra,xa->srx/dot_general | solution.py:83
  31.9 14.1 %fusion.56 = f32[2,16,32,8,128]{4,2,3,0,1:T(8,128)S(1)} fusion(f32[2,128,8,512]{3,1,2,0:T(8,128)S(1)} %fusion.6, f32[2,128,8,512]{3,2,1,0:T(8,128)S(1)} %copy-done.3, s32[16,32]{1,0:T(8,128)S(1)} %multiply_add_fusion.3), kind=kOutput, calls=%fused_computation.68 | convolution fusion | flops 6451888128 | bytes 12584960 | tf_op jit(solution)/shard_map/scdx,xqk->sqkdc/dot_general | solution.py:121
  46.0 5.8 %copy.87 = f32[2,16,32,8,128]{4,3,2,1,0:T(8,128)} copy(f32[2,16,32,8,128]{4,2,3,0,1:T(8,128)S(1)} %fusion.56) | data formatting | bytes 8388608 | tf_op jit(solution)/shard_map/scdx,xqk->sqkdc/transpose | solution.py:121
  51.8 4.9 reshape.412
  56.8 2.6 fusion.235
  59.4 2.5 fusion.234
  61.9 2.5 fusion.233
  64.4 2.5 fusion.232
  66.9 2.5 fusion.231
  69.4 2.5 fusion.230
  72.0 2.5 fusion.229
  74.5 2.5 fusion.228
  77.0 0.8 fusion.227
  77.8 0.9 fusion.226
  78.8 0.9 fusion.225
  79.7 0.9 fusion.224
  80.6 0.9 fusion.223
  81.5 0.9 fusion.222
  82.5 0.9 fusion.221
  83.4 0.9 fusion.220
  84.3 7.2 %all-to-all-start = ((f32[16,2,1,1,32768]{4,2,3,1,0:T(1,128)}), f32[16,2,1,1,32768]{4,2,3,1,0:T(1,128)}, u32[]{:S(2)}, u32[]{:S(2)}) async-start(f32[16,2,1,1,32768]{4,2,3,1,0:T(1,128)} %fusion.220), calls=%async_computation | async-start | bytes 8388608 | tf_op jit(solution)/shard_map/all_to_all | solution.py:126
  98.3 70.3 %all-to-all-done = f32[16,2,1,1,32768]{4,2,3,1,0:T(1,128)} async-done(((f32[16,2,1,1,32768]{4,2,3,1,0:T(1,128)}), f32[16,2,1,1,32768]{4,2,3,1,0:T(1,128)}, u32[]{:S(2)}, u32[]{:S(2)}) %all-to-all-start) | async-done | bytes 4194336 | tf_op jit(solution)/shard_map/all_to_all | solution.py:126
  168.6 13.7 %fusion.23 = f32[2,4,32,8,512,1]{4,3,5,1,2,0:T(8,128)S(1)} fusion(f32[2,4,4,32,8,128]{5,4,3,0,2,1:T(8,128)} %bitcast.55, s32[4,128]{1,0:T(4,128)S(1)} %multiply_add_fusion.5), kind=kOutput, calls=%fused_computation.28 | convolution fusion | flops 6446645248 | bytes 8390656 | tf_op jit(solution)/shard_map/sabxdc,acy->sbxdy/dot_general | solution.py:130
  182.4 4.3 fusion.59
  186.7 10.6 %fusion.90 = f32[1,32,32,512]{3,2,1,0:T(8,128)S(1)} fusion(f32[2,32,32,512]{3,2,1,0:T(8,128)S(1)} %fusion.59, f32[]{:T(128)} %bitcast.14, f32[]{:T(128)} %bitcast.13, f32[]{:T(128)} %bitcast.12, f32[]{:T(128)} %bitcast.11, f32[]{:T(128)} %bitcast.10, f32[]{:T(128)} %bitcast.9, f32[]{:T(128)} %bitcast.8, f32[512]{0:T(512)S(1)} %fusion.256, ...), kind=kLoop, calls=%fused_computation.96 | loop fusion | flops 31457280 | bytes 6297648 | tf_op jit(solution)/shard_map/stack | solution.py:59
  197.3 13.0 %fusion.101 = f32[1,32,32,512]{3,2,1,0:T(8,128)S(1)} fusion(f32[2,32,32,512]{3,2,1,0:T(8,128)S(1)} %fusion.59, f32[]{:T(128)} %bitcast.74, f32[]{:T(128)} %bitcast.73, f32[]{:T(128)} %bitcast.72, f32[]{:T(128)} %bitcast.71, f32[]{:T(128)} %bitcast.14, f32[]{:T(128)} %bitcast.12, f32[]{:T(128)} %bitcast.10, f32[]{:T(128)} %bitcast.8, f32[512]{0:T(512)S(1)} %fusion.256, ...), kind=kLoop, calls=%fused_computation.107 | loop fusion | flops 50331648 | bytes 6297648 | tf_op jit(solution)/shard_map/stack | solution.py:59
  210.3 4.1 fusion.62
  214.4 13.6 %fusion.63 = f32[2,4,4,32,8,128]{5,3,4,2,0,1:T(8,128)S(1)} fusion(f32[2,32,4,8,512]{4,3,1,0,2:T(8,128)S(1)} %fusion.62, s32[4,128]{1,0:T(4,128)S(1)} %multiply_add_fusion.5), kind=kOutput, calls=%fused_computation.71 | convolution fusion | flops 6446645248 | bytes 8390656 | tf_op jit(solution)/shard_map/sxbdy,acy->sabxdc/dot_general | solution.py:142
  227.9 5.8 %copy.138 = f32[2,4,4,32,8,128]{5,4,3,0,2,1:T(8,128)} copy(f32[2,4,4,32,8,128]{5,3,4,2,0,1:T(8,128)S(1)} %fusion.63) | data formatting | bytes 8388608 | tf_op jit(solution)/shard_map/reshape | solution.py:143
  233.8 5.9 %reshape.435 = f32[2,16,1,32768]{3,0,2,1:T(2,128)} reshape(f32[2,4,4,32,8,128]{5,4,3,0,2,1:T(8,128)} %copy.138) | data formatting | bytes 8388608 | tf_op jit(solution)/shard_map/reshape | solution.py:143
  239.7 19.7 %all-to-all-start.1 = ((f32[2,16,1,32768]{3,0,2,1:T(2,128)}), f32[2,16,1,32768]{3,0,2,1:T(2,128)}, u32[]{:S(2)}, u32[]{:S(2)}) async-start(f32[2,16,1,32768]{3,0,2,1:T(2,128)} %reshape.435), calls=%async_computation.1 | async-start | bytes 8388608 | tf_op jit(solution)/shard_map/all_to_all | solution.py:145
  259.4 18.3 %copy.114 = f32[4,2,128,8,512]{2,0,3,4,1:T(4,128)} copy(f32[4,2,128,8,512]{4,3,2,1,0:T(8,128)} %param.10) | data formatting | bytes 33554432 | tf_op args[2]
  277.7 17.5 %multiply_add_fusion = f32[4,2,128,8,512]{4,3,2,1,0:T(8,128)} fusion(f32[4,2,128,8,512]{4,3,2,1,0:T(8,128)} %param.9, f32[4,2,128,8,512]{4,3,2,1,0:T(8,128)} %param.10), kind=kLoop, calls=%fused_computation.6 | loop fusion | flops 8388608 | bytes 50331648 | tf_op jit(solution)/shard_map/add | solution.py:159
  295.2 41.7 %all-to-all-done.1 = f32[2,16,1,32768]{3,0,2,1:T(2,128)} async-done(((f32[2,16,1,32768]{3,0,2,1:T(2,128)}), f32[2,16,1,32768]{3,0,2,1:T(2,128)}, u32[]{:S(2)}, u32[]{:S(2)}) %all-to-all-start.1) | async-done | bytes 4194336 | tf_op jit(solution)/shard_map/all_to_all | solution.py:145
  336.9 6.6 %reshape.436 = f32[2,16,32,8,128]{4,3,2,0,1:T(8,128)} reshape(f32[2,16,1,32768]{3,0,2,1:T(2,128)} %all-to-all-done.1) | data formatting | bytes 8388608 | tf_op jit(solution)/shard_map/reshape | solution.py:147
  343.5 26.4 %fusion.14 = f32[2,128,8,512]{3,1,2,0:T(8,128)S(1)} fusion(f32[2,128,8,512]{3,2,1,0:T(8,128)} %param.8, f32[2,128,8,512]{3,1,2,0:T(8,128)} %copy-done.7, f32[2,16,32,8,128]{4,3,2,0,1:T(8,128)} %reshape.436, s32[16,32]{1,0:T(8,128)S(1)} %multiply_add_fusion.3), kind=kOutput, calls=%fused_computation.18 | convolution fusion | flops 6453985280 | bytes 16779264 | tf_op jit(solution)/shard_map/sqxdc,qxk->scdk/dot_general | solution.py:148
  369.9 4.4 copy.120
  374.4 11.0 %copy.113 = f32[1,2,128,8,512]{2,0,3,4,1:T(1,128)} copy(f32[1,2,128,8,512]{4,2,3,1,0:T(8,128)} %bitcast.232) | data formatting | bytes 8388608 | tf_op jit(solution)/shard_map/broadcast_in_dim | solution.py:150
  385.4 76.1 %fusion.132 = f32[5,5]{0,1:T(8,128)S(1)} fusion(f32[4,2,128,8,512]{2,0,3,4,1:T(4,128)} %copy.114, f32[1,2,128,8,512]{2,0,3,4,1:T(1,128)} %copy.113), kind=kOutput, calls=%fused_computation.158 | convolution fusion | flops 319815680 | bytes 20971620 | tf_op jit(solution)/shard_map/isyzx,jsyzx->ij/dot_general | solution.py:151
  461.4 47.7 %psum.7 = f32[5,5]{0,1:T(8,128)S(1)} all-reduce(f32[5,5]{0,1:T(8,128)S(1)} %fusion.132), channel_id=1, replica_groups=mesh['groups'=2,'gy'=4,'gz'=4] {'gy','gz'}, use_global_device_ids=true, to_apply=%region_0.2 | all-reduce | flops 25 | bytes 200 | tf_op jit(solution)/shard_map/psum | solution.py:152
  513.0 46.8 %fusion.4 = f32[1,2,128,8,512]{4,0,3,2,1:T(1,128)S(1)} fusion(f32[4,2,128,8,512]{4,3,2,1,0:T(8,128)} %multiply_add_fusion, f32[5]{0:T(128)S(1)} %broadcast_divide_fusion), kind=kOutput, calls=%fused_computation.4 | convolution fusion | flops 50331648 | bytes 20971540 | tf_op jit(solution)/shard_map/i,isyzx->syzx/dot_general | solution.py:158
  559.8 5.1 bitcast_add_fusion
  565.0 4.4 copy.119
  (55 shorter events, 7.3 us)
Async XLA Ops:
  2.7 6.7 %collective-permute-start = (f32[5,1,1,128]{3,2,1,0:T(1,128)S(1)}, f32[5,1,1,128]{3,2,1,0:T(1,128)S(1)}, u32[]{:S(2)}, u32[]{:S(2)}) collective-permute-start(f32[5,1,1,128]{3,2,1,0:T(1,128)S(1)} %pad_maximum_fusion.5), channel_id=1, source_target_pairs={{0,4},{4,8},{8,12},{12,0},{1,5},{5,9},{9,13},{13,1},{2,6},{6,10},{... | collective-permute-start | bytes 7688 | tf_op jit(solution)/shard_map/ppermute | solution.py:21
  5.7 3.6 collective-permute-start.1
  9.3 3.1 collective-permute-start.2
  9.4 3.1 collective-permute-start.3
  13.1 18.8 %copy-start.3 = (f32[2,128,8,512]{3,2,1,0:T(8,128)S(1)}, f32[2,128,8,512]{3,2,1,0:T(8,128)}, u32[]{:S(2)}) copy-start(f32[2,128,8,512]{3,2,1,0:T(8,128)} %param.8) | copy-start | bytes 12582916
  31.9 14.1 %copy-start.7 = (f32[2,128,8,512]{3,1,2,0:T(8,128)}, f32[2,128,8,512]{3,1,2,0:T(8,128)S(1)}, u32[]{:S(2)}) copy-start(f32[2,128,8,512]{3,1,2,0:T(8,128)S(1)} %fusion.6) | copy-start | bytes 12582916
  56.8 20.2 %copy-start.2 = (f32[2,16,1,32768]{3,1,0,2:T(8,128)S(1)}, f32[2,16,1,32768]{3,1,0,2:T(8,128)}, u32[]{:S(2)}) copy-start(f32[2,16,1,32768]{3,1,0,2:T(8,128)} %reshape.412) | copy-start | bytes 12582916
  84.3 7.2 %copy-start.6 = (f32[4]{0:T(128)S(1)}, f32[4]{0:T(128)}, u32[]{:S(2)}) copy-start(f32[4]{0:T(128)} %param.14) | copy-start | bytes 52
  84.3 13.2 %copy-start.5 = (f32[3,4]{1,0:T(4,128)S(1)}, f32[3,4]{1,0:T(4,128)}, u32[]{:S(2)}) copy-start(f32[3,4]{1,0:T(4,128)} %param.13) | copy-start | bytes 148
  84.3 84.3 %all-to-all-start = ((f32[16,2,1,1,32768]{4,2,3,1,0:T(1,128)}), f32[16,2,1,1,32768]{4,2,3,1,0:T(1,128)}, u32[]{:S(2)}, u32[]{:S(2)}) async-start(f32[16,2,1,1,32768]{4,2,3,1,0:T(1,128)} %fusion.220), calls=%async_computation | async-start | bytes 8388608 | tf_op jit(solution)/shard_map/all_to_all | solution.py:126
  239.7 97.2 %all-to-all-start.1 = ((f32[2,16,1,32768]{3,0,2,1:T(2,128)}), f32[2,16,1,32768]{3,0,2,1:T(2,128)}, u32[]{:S(2)}, u32[]{:S(2)}) async-start(f32[2,16,1,32768]{3,0,2,1:T(2,128)} %reshape.435), calls=%async_computation.1 | async-start | bytes 8388608 | tf_op jit(solution)/shard_map/all_to_all | solution.py:145
  369.9 4.5 copy-start
  513.0 46.8 %copy-start.1 = (f32[2,128,8,512]{3,1,2,0:T(8,128)S(1)}, f32[2,128,8,512]{3,1,2,0:T(8,128)}, u32[]{:S(2)}) copy-start(f32[2,128,8,512]{3,1,2,0:T(8,128)} %copy-done) | copy-start | bytes 12582916
  513.0 46.8 %copy-start.4 = (f32[2,128,8,512]{3,2,1,0:T(8,128)S(1)}, f32[2,128,8,512]{3,2,1,0:T(8,128)}, u32[]{:S(2)}) copy-start(f32[2,128,8,512]{3,2,1,0:T(8,128)} %param.8) | copy-start | bytes 12582916
